TPU v7x, 32 devices: a whole 2x2x4 slice. The times are simulated.
32 devices in a mesh: group: 2 (over y), seq: 4 (over z), head: 4 (over x, core).
Axes of the slice: x: 2, y: 2, z: 4, core: 2. Of those that a mesh axis runs over, the one named last changes fastest.
Arguments:
- q_lin: bfloat16 [3072, 2048], P(('group', 'seq'), 'head'), parts along dimension 0, may hold values from -6 to 6
- k_lin: bfloat16 [3072, 2048], P(('group', 'seq'), 'head'), parts along dimension 0, may hold values from -6 to 6
- v_lin: bfloat16 [3072, 2048], P(('group', 'seq'), 'head'), parts along dimension 0, may hold values from -6 to 6
- q_soft: bfloat16 [3072, 2048], P(('group', 'seq'), 'head'), parts along dimension 0, may hold values from -5 to 5
- k_soft: bfloat16 [3072, 2048], P(('group', 'seq'), 'head'), parts along dimension 0, may hold values from -5 to 5
- v_soft: bfloat16 [3072, 2048], P(('group', 'seq'), 'head'), parts along dimension 0, may hold values from -6 to 6
- segment: int32 [3072], P(('group', 'seq')), parts along dimension 0, may hold values from 0 to 3, as said below
Outputs:
- mixed_lin: bfloat16 [3072, 2048], P(('group', 'seq'), 'head'), parts along dimension 0
- mixed_soft: bfloat16 [3072, 2048], P(('group', 'seq'), 'head'), parts along dimension 0
There are 2 independent parts, one for each index of `group`. A program takes and returns all parts, laid end to end along the dimension named above; each array names one. Nothing has to cross between parts.
Inputs may be any that keep to these rules, and one draw needn't show every extreme that they name: `segment`: document numbers never fall along the list; each of the 4 documents has 1 to 960 tokens and one has exactly 960.
All inputs are finite; a program needn't handle non-finite values.
Results may differ from a plain program's by a relative error of at most 0.0075.
Values may be sent and summed in bfloat16 or wider, within the bound.
A program may use at most 128 MiB of HBM per device.

v0:
```python
import jax
import jax.numpy as jnp
from jax import lax
from jax.sharding import PartitionSpec as P

HEAD_DIM = 128


def entering(shard, axis, combine, identity):
    devices, position = (lax.axis_size(axis), lax.axis_index(axis))
    everything = jax.tree.map(
        lambda part, kind: lax.all_gather(part.astype(kind), axis),
        shard,
        (jnp.bfloat16, jnp.bfloat16),
    )
    start = jax.tree.map(
        lambda part, zero: jnp.broadcast_to(jnp.asarray(zero, part.dtype), part.shape),
        shard,
        identity,
    )

    def hop(k, before):
        reached = k < position
        new = combine(
            before, jax.tree.map(lambda part, own: part[k].astype(own.dtype), everything, shard)
        )
        return jax.tree.map(lambda a, b: jnp.where(reached, a, b), new, before)

    return lax.fori_loop(0, devices, hop, start)


def shifted(value, axis, steps):
    count = lax.axis_size(axis)
    initial, last = (max(0, -steps), min(count, count - steps))
    return lax.ppermute(value, axis, [(source, source + steps) for source in range(initial, last)])


def join_states(earlier, later):
    early_state, early_last = earlier
    late_state, late_last = later
    joined = late_state + jnp.where(early_last == late_last, early_state, 0.0)
    memory_state = jnp.where(late_last < 0.0, early_state, joined)
    last_id = jnp.where(late_last < 0.0, early_last, late_last)
    return (memory_state, last_id)


def on_device(q_lin, k_lin, v_lin, q_soft, k_soft, v_soft, segment):
    rows = q_lin.shape[0]
    heads_here = q_lin.shape[1] // HEAD_DIM
    shape = (rows, heads_here, HEAD_DIM)
    single_query = q_lin.reshape(shape)
    single_key = k_lin.reshape(shape)
    single_value = v_lin.reshape(shape)
    places = jnp.arange(rows, dtype=jnp.int32)
    me_index = lax.axis_index("seq")
    scores = jnp.einsum(
        "thd,shd->hts", single_query, single_key, preferred_element_type=jnp.float32
    )
    same = (segment[:, None] == segment[None, :]) & (places[:, None] >= places[None, :])
    scores = jnp.where(same[None], scores, 0.0)
    inner = jnp.einsum(
        "hts,shd->thd", scores, single_value.astype(jnp.float32), precision=lax.Precision.HIGHEST
    )
    retain_mask = (segment == segment[-1]).astype(single_key.dtype)
    local_state = jnp.einsum(
        "piy,piw->iyw",
        single_key * retain_mask[:, None, None],
        single_value,
        preferred_element_type=jnp.float32,
    )
    own_last = segment[-1].astype(jnp.float32)
    empty = jnp.zeros((heads_here, HEAD_DIM, HEAD_DIM), jnp.float32)
    arriving_state, carried = entering(
        (local_state, own_last), "seq", join_states, (empty, jnp.float32(-1.0))
    )
    apply = (segment.astype(jnp.float32) == carried).astype(jnp.float32)
    outer_product = jnp.einsum(
        "upi,pis->ups",
        single_query.astype(jnp.float32),
        arriving_state,
        precision=lax.Precision.HIGHEST,
    )
    raw = inner + outer_product * apply[:, None, None]
    normed = raw * lax.rsqrt(jnp.mean(raw * raw, axis=-1, keepdims=True) + 1e-06)
    mixed_lin = normed.reshape(rows, heads_here * HEAD_DIM).astype(jnp.bfloat16)
    q_heads = q_soft.reshape(shape)
    q_pos = me_index * rows + places
    scale = HEAD_DIM ** (-0.5)

    def attend(carry, piece, start):
        keys, values, ids = piece
        count = keys.shape[0] // rows
        key_blocks = keys.reshape(count, rows, heads_here, HEAD_DIM)
        value_blocks = values.reshape(count, rows, heads_here, HEAD_DIM)
        id_blocks = ids.reshape(count, rows).astype(jnp.int32)
        offsets = start + rows * jnp.arange(count, dtype=jnp.int32)

        def one_block(memory_state, block_in):
            key_block_slice, value_block_slice, id_blk, offset = block_in
            top, total, accum = memory_state
            logits = (
                jnp.einsum(
                    "thd,shd->hts", q_heads, key_block_slice, preferred_element_type=jnp.float32
                )
                * scale
            )
            key_pos = offset + places
            mask = (
                (key_pos[None, :] <= q_pos[:, None])
                & (key_pos[None, :] >= 0)
                & (id_blk[None, :] == segment[:, None])
            )
            new_top = jnp.maximum(top, jnp.max(jnp.where(mask[None], logits, -1e30), axis=-1))
            factor = jnp.exp(top - new_top)
            expo = jnp.where(mask[None], jnp.exp(logits - new_top[..., None]), 0.0)
            total = total * factor + jnp.sum(expo, axis=-1)
            added = jnp.einsum(
                "hts,shd->thd",
                expo.astype(jnp.bfloat16),
                value_block_slice,
                preferred_element_type=jnp.float32,
            )
            accum = accum * factor.T[:, :, None] + added
            memory_state = (new_top, total, accum)
            return (memory_state, None)

        carry, _ = lax.scan(one_block, carry, (key_blocks, value_blocks, id_blocks, offsets))
        return carry

    start_state = (
        jnp.full((heads_here, rows), -1e30, jnp.float32),
        jnp.zeros((heads_here, rows), jnp.float32),
        jnp.zeros(shape, jnp.float32),
    )
    ids_wire = segment.astype(jnp.bfloat16)
    seq_count = lax.axis_size("seq")
    longest = rows * seq_count * 5 // 8
    reach_steps = min(seq_count - 1, (longest - 2) // rows + 1)
    first_state = attend(start_state, (k_soft, v_soft, ids_wire), me_index * rows)

    def forward(step, loop_carry):
        memory_state, keys, values, ids = loop_carry
        keys, values, ids = shifted((keys, values, ids), "seq", 1)
        memory_state = attend(memory_state, (keys, values, ids), (me_index - step) * rows)
        return (memory_state, keys, values, ids)

    final_carry = lax.fori_loop(
        1, reach_steps + 1, forward, (first_state, k_soft, v_soft, ids_wire)
    )
    top, total, accum = final_carry[0]
    mixed_soft = (
        (accum / total.T[:, :, None]).reshape(rows, heads_here * HEAD_DIM).astype(jnp.bfloat16)
    )
    return (mixed_lin, mixed_soft)


def solution(mesh):
    in_specs = (
        P(("group", "seq"), "head"),
        P(("group", "seq"), "head"),
        P(("group", "seq"), "head"),
        P(("group", "seq"), "head"),
        P(("group", "seq"), "head"),
        P(("group", "seq"), "head"),
        P(("group", "seq")),
    )
    out_specs = (P(("group", "seq"), "head"), P(("group", "seq"), "head"))
    return jax.shard_map(
        on_device, mesh=mesh, in_specs=in_specs, out_specs=out_specs, check_vma=False
    )
```

profile of v0, /device:TPU:0, one launch (start us, length us, event | category | flops | bytes accessed | tf_op | source)
XLA Modules:
  0.0 129.4 jit_solution(17783946946622038517)
XLA Ops:
  0.6 0.0 copy-start
  0.7 0.7 fusion.56
  1.4 1.1 compare_and_fusion.1
  2.5 1.2 copy.50
  3.7 1.7 %select_reduce_fusion.1 = (f32[4,384]{1,0:T(4,128)S(1)}, f32[4,384,384]{2,1,0:T(8,128)S(1)}) fusion(pred[384,384]{1,0:T(8,128)(4,1)S(1)} %get-tuple-element.531, bf16[384,4,128]{0,2,1:T(8,128)(2,1)S(1)} %bitcast.106, bf16[384,512]{1,0:T(8,128)(2,1)} %param.15), kind=kOutput, calls=%fused_computation.24 | convolution fusion | flops 152762880 | bytes 3299328 | tf_op jit(solution)/shard_map/while/body/eval_jaxpr/thd,shd->hts/dot_general | solution.py:102
  5.5 0.9 fusion.18
  6.4 0.8 fusion.21
  7.2 0.2 copy.57
  7.4 0.2 copy.55
  7.7 0.9 copy.56
  8.6 75.5 %while.60 = (s32[]{:T(128)}, f32[4,384]{1,0:T(4,128)S(1)}, f32[4,384]{1,0:T(4,128)S(1)}, f32[384,4,128]{2,0,1:T(8,128)S(1)}, bf16[384,512]{0,1:T(8,128)(2,1)S(1)...) while((s32[]{:T(128)}, f32[4,384]{1,0:T(4,128)S(1)}, ...), condition=%wide.region_8.9_spmd.clone, body=%wide.region_5.8_spmd.clone.sunk | while | flops 309467520 | bytes 15254297 | solution.py:147
  8.6 5.1 %collective-permute-start = (bf16[384]{0:T(512)(128)(2,1)S(1)}, bf16[384]{0:T(512)(128)(2,1)S(1)}, u32[]{:S(2)}, u32[]{:S(2)}) collective-permute-start(bf16[384]{0:T(512)(128)(2,1)S(1)} %get-tuple-element.699), channel_id=1, source_target_pairs={{0,4},{4,8},{8,12},{1,5},{5,9},{9,13},{2,6},{6,10},{10,14},{3,7},{... | collective-permute-start | bytes 2312 | tf_op jit(solution)/shard_map/while/body/eval_jaxpr/ppermute | solution.py:35
  13.7 3.5 %collective-permute-start.1 = (bf16[384,512]{0,1:T(8,128)(2,1)S(1)}, bf16[384,512]{0,1:T(8,128)(2,1)S(1)}, u32[]{:S(2)}, u32[]{:S(2)}) collective-permute-start(bf16[384,512]{0,1:T(8,128)(2,1)S(1)} %get-tuple-element.697), channel_id=1, source_target_pairs={{0,4},{4,8},{8,12},{1,5},{5,9},{9,13},{2,6},{6,10},{10,14},{3,7},{... | collective-permute-start | bytes 1179656 | tf_op jit(solution)/shard_map/while/body/eval_jaxpr/ppermute | solution.py:35
  17.2 3.5 %collective-permute-start.2 = (bf16[384,512]{0,1:T(8,128)(2,1)}, bf16[384,512]{0,1:T(8,128)(2,1)S(1)}, u32[]{:S(2)}, u32[]{:S(2)}) collective-permute-start(bf16[384,512]{0,1:T(8,128)(2,1)} %get-tuple-element.698), channel_id=1, source_target_pairs={{0,4},{4,8},{8,12},{1,5},{5,9},{9,13},{2,6},{6,10},{10,14},{3,7},{... | collective-permute-start | bytes 1179656 | tf_op jit(solution)/shard_map/while/body/eval_jaxpr/ppermute | solution.py:35
  20.7 0.2 compare_and_fusion.3
  21.0 5.7 %collective-permute-done.1 = bf16[384,512]{0,1:T(8,128)(2,1)S(1)} collective-permute-done((bf16[384,512]{0,1:T(8,128)(2,1)S(1)}, bf16[384,512]{0,1:T(8,128)(2,1)S(1)}, u32[]{:S(2)}, u32[]{:S(2)}) %collective-permute-start.1) | collective-permute-done | bytes 393248 | tf_op jit(solution)/shard_map/while/body/eval_jaxpr/ppermute | solution.py:35
  26.7 0.6 select_reduce_fusion.3
  27.3 0.5 fusion.82
  27.8 5.9 %collective-permute-done.2 = bf16[384,512]{0,1:T(8,128)(2,1)S(1)} collective-permute-done((bf16[384,512]{0,1:T(8,128)(2,1)}, bf16[384,512]{0,1:T(8,128)(2,1)S(1)}, u32[]{:S(2)}, u32[]{:S(2)}) %collective-permute-start.2) | collective-permute-done | bytes 393248 | tf_op jit(solution)/shard_map/while/body/eval_jaxpr/ppermute | solution.py:35
  33.8 1.1 fusion.83
  34.9 0.7 copy.130
  35.7 4.3 %collective-permute-start = (bf16[384]{0:T(512)(128)(2,1)S(1)}, bf16[384]{0:T(512)(128)(2,1)S(1)}, u32[]{:S(2)}, u32[]{:S(2)}) collective-permute-start(bf16[384]{0:T(512)(128)(2,1)S(1)} %get-tuple-element.699), channel_id=1, source_target_pairs={{0,4},{4,8},{8,12},{1,5},{5,9},{9,13},{2,6},{6,10},{10,14},{3,7},{... | collective-permute-start | bytes 2312 | tf_op jit(solution)/shard_map/while/body/eval_jaxpr/ppermute | solution.py:35
  39.9 3.5 %collective-permute-start.1 = (bf16[384,512]{0,1:T(8,128)(2,1)S(1)}, bf16[384,512]{0,1:T(8,128)(2,1)S(1)}, u32[]{:S(2)}, u32[]{:S(2)}) collective-permute-start(bf16[384,512]{0,1:T(8,128)(2,1)S(1)} %get-tuple-element.697), channel_id=1, source_target_pairs={{0,4},{4,8},{8,12},{1,5},{5,9},{9,13},{2,6},{6,10},{10,14},{3,7},{... | collective-permute-start | bytes 1179656 | tf_op jit(solution)/shard_map/while/body/eval_jaxpr/ppermute | solution.py:35
  43.5 2.2 %collective-permute-start.2 = (bf16[384,512]{0,1:T(8,128)(2,1)}, bf16[384,512]{0,1:T(8,128)(2,1)S(1)}, u32[]{:S(2)}, u32[]{:S(2)}) collective-permute-start(bf16[384,512]{0,1:T(8,128)(2,1)} %get-tuple-element.698), channel_id=1, source_target_pairs={{0,4},{4,8},{8,12},{1,5},{5,9},{9,13},{2,6},{6,10},{10,14},{3,7},{... | collective-permute-start | bytes 1179656 | tf_op jit(solution)/shard_map/while/body/eval_jaxpr/ppermute | solution.py:35
  45.7 0.2 compare_and_fusion.3
  46.0 7.0 %collective-permute-done.1 = bf16[384,512]{0,1:T(8,128)(2,1)S(1)} collective-permute-done((bf16[384,512]{0,1:T(8,128)(2,1)S(1)}, bf16[384,512]{0,1:T(8,128)(2,1)S(1)}, u32[]{:S(2)}, u32[]{:S(2)}) %collective-permute-start.1) | collective-permute-done | bytes 393248 | tf_op jit(solution)/shard_map/while/body/eval_jaxpr/ppermute | solution.py:35
  52.9 0.6 select_reduce_fusion.3
  53.6 0.5 fusion.82
  54.1 4.8 %collective-permute-done.2 = bf16[384,512]{0,1:T(8,128)(2,1)S(1)} collective-permute-done((bf16[384,512]{0,1:T(8,128)(2,1)}, bf16[384,512]{0,1:T(8,128)(2,1)S(1)}, u32[]{:S(2)}, u32[]{:S(2)}) %collective-permute-start.2) | collective-permute-done | bytes 393248 | tf_op jit(solution)/shard_map/while/body/eval_jaxpr/ppermute | solution.py:35
  58.9 1.1 fusion.83
  60.1 0.7 copy.130
  60.8 4.3 %collective-permute-start = (bf16[384]{0:T(512)(128)(2,1)S(1)}, bf16[384]{0:T(512)(128)(2,1)S(1)}, u32[]{:S(2)}, u32[]{:S(2)}) collective-permute-start(bf16[384]{0:T(512)(128)(2,1)S(1)} %get-tuple-element.699), channel_id=1, source_target_pairs={{0,4},{4,8},{8,12},{1,5},{5,9},{9,13},{2,6},{6,10},{10,14},{3,7},{... | collective-permute-start | bytes 2312 | tf_op jit(solution)/shard_map/while/body/eval_jaxpr/ppermute | solution.py:35
  65.1 2.5 %collective-permute-start.1 = (bf16[384,512]{0,1:T(8,128)(2,1)S(1)}, bf16[384,512]{0,1:T(8,128)(2,1)S(1)}, u32[]{:S(2)}, u32[]{:S(2)}) collective-permute-start(bf16[384,512]{0,1:T(8,128)(2,1)S(1)} %get-tuple-element.697), channel_id=1, source_target_pairs={{0,4},{4,8},{8,12},{1,5},{5,9},{9,13},{2,6},{6,10},{10,14},{3,7},{... | collective-permute-start | bytes 1179656 | tf_op jit(solution)/shard_map/while/body/eval_jaxpr/ppermute | solution.py:35
  67.6 2.2 %collective-permute-start.2 = (bf16[384,512]{0,1:T(8,128)(2,1)}, bf16[384,512]{0,1:T(8,128)(2,1)S(1)}, u32[]{:S(2)}, u32[]{:S(2)}) collective-permute-start(bf16[384,512]{0,1:T(8,128)(2,1)} %get-tuple-element.698), channel_id=1, source_target_pairs={{0,4},{4,8},{8,12},{1,5},{5,9},{9,13},{2,6},{6,10},{10,14},{3,7},{... | collective-permute-start | bytes 1179656 | tf_op jit(solution)/shard_map/while/body/eval_jaxpr/ppermute | solution.py:35
  69.9 0.2 compare_and_fusion.3
  70.1 7.0 %collective-permute-done.1 = bf16[384,512]{0,1:T(8,128)(2,1)S(1)} collective-permute-done((bf16[384,512]{0,1:T(8,128)(2,1)S(1)}, bf16[384,512]{0,1:T(8,128)(2,1)S(1)}, u32[]{:S(2)}, u32[]{:S(2)}) %collective-permute-start.1) | collective-permute-done | bytes 393248 | tf_op jit(solution)/shard_map/while/body/eval_jaxpr/ppermute | solution.py:35
  77.1 0.6 select_reduce_fusion.3
  77.7 0.5 fusion.82
  78.3 4.0 %collective-permute-done.2 = bf16[384,512]{0,1:T(8,128)(2,1)S(1)} collective-permute-done((bf16[384,512]{0,1:T(8,128)(2,1)}, bf16[384,512]{0,1:T(8,128)(2,1)S(1)}, u32[]{:S(2)}, u32[]{:S(2)}) %collective-permute-start.2) | collective-permute-done | bytes 393248 | tf_op jit(solution)/shard_map/while/body/eval_jaxpr/ppermute | solution.py:35
  82.2 1.1 fusion.83
  83.4 0.7 copy.130
  84.1 1.0 copy_bitcast_fusion
  85.1 0.2 copy.66
  85.4 0.4 fusion.41
  85.8 1.6 %fusion.22 = f32[384,4,128]{0,2,1:T(8,128)S(1)} fusion(f32[4,384,384]{2,1,0:T(8,128)S(1)} %fusion.41, pred[384,384]{1,0:T(8,128)(4,1)S(1)} %get-tuple-element.532, bf16[384,512]{1,0:T(8,128)(2,1)S(1)} %copy-done.2), kind=kOutput, calls=%fused_computation.34 | convolution fusion | flops 906559488 | bytes 3686400 | tf_op jit(solution)/shard_map/hts,shd->thd/dot_general | solution.py:61
  87.5 0.6 slice.4
  88.1 0.6 compare_convert_fusion
  88.7 0.3 convolution_convert_fusion
  89.0 15.7 %all-gather = bf16[16,128,128]{2,1,0:T(8,128)(2,1)S(1)} all-gather(bf16[4,128,128]{2,1,0:T(8,128)(2,1)S(1)} %convolution_convert_fusion), channel_id=2, replica_groups=mesh['group'=2,'seq'=4,'head'=4] {'seq'}, dimensions={0}, use_global_device_ids=true | all-gather | bytes 655360 | tf_op jit(solution)/shard_map/all_gather | solution.py:12
  104.7 0.6 dynamic-slice
  106.0 0.7 dynamic-update-slice
  106.7 9.9 %all-reduce = bf16[4]{0:T(256)(128)(2,1)S(1)} all-reduce(bf16[4]{0:T(256)(128)(2,1)S(1)} %dynamic-update-slice), channel_id=1, replica_groups=mesh['group'=2,'seq'=4,'head'=4] {'seq'}, use_global_device_ids=true, to_apply=%add | all-reduce | flops 4 | bytes 16
  116.5 11.2 %while.61 = (s32[]{:T(128)}, f32[4,128,128]{2,1,0:T(8,128)S(1)}, f32[]{:T(128)}, s32[]{:T(128)}, bf16[4]{0:T(256)(128)(2,1)S(1)}, /*index=5*/bf16[4,4,128,128]{3...) while((s32[]{:T(128)}, f32[4,128,128]{2,1,0:T(8,128)S(1)}, f32[]{:T(128)}, s32[]{:T(128)}, ...), condition=%wide.region_1.2_spmd.clone, body=%wide.region_0.1_spmd.clone.sunk | while | flops 393224 | bytes 655525 | solution.py:29
  116.6 0.7 dynamic_slice.47
  118.5 0.2 select_select_fusion.2
  119.4 0.7 dynamic_slice.47
  121.3 0.2 select_select_fusion.2
  122.1 0.7 dynamic_slice.47
  124.1 0.2 select_select_fusion.2
  124.9 0.7 dynamic_slice.47
  126.9 0.2 select_select_fusion.2
  127.7 0.6 multiply_reduce_fusion
  128.4 0.1 multiply_convert_fusion
  128.5 0.9 copy.59
  (48 shorter events, 0.4 us)
Async XLA Ops:
  0.6 84.7 %copy-start = (bf16[384,512]{1,0:T(8,128)(2,1)S(1)}, bf16[384,512]{1,0:T(8,128)(2,1)}, u32[]{:S(2)}) copy-start(bf16[384,512]{1,0:T(8,128)(2,1)} %param.11) | copy-start | bytes 1179652
  3.7 2.7 %copy-start.3 = (bf16[384,512]{1,0:T(8,128)(2,1)S(1)}, bf16[384,512]{1,0:T(8,128)(2,1)}, u32[]{:S(2)}) copy-start(bf16[384,512]{1,0:T(8,128)(2,1)} %param.16) | copy-start | bytes 1179652
  6.4 1.0 copy-start.1
  7.2 1.4 %copy-start.5 = (s32[384]{0:T(512)S(1)}, s32[384]{0:T(512)}, u32[]{:S(2)}) copy-start(s32[384]{0:T(512)} %param.17) | copy-start | bytes 4612
  8.6 76.6 %copy-start.4 = (bf16[384,512]{1,0:T(8,128)(2,1)S(1)}, bf16[384,512]{1,0:T(8,128)(2,1)}, u32[]{:S(2)}) copy-start(bf16[384,512]{1,0:T(8,128)(2,1)} %param.12) | copy-start | bytes 1179652
  8.6 12.1 %collective-permute-start = (bf16[384]{0:T(512)(128)(2,1)S(1)}, bf16[384]{0:T(512)(128)(2,1)S(1)}, u32[]{:S(2)}, u32[]{:S(2)}) collective-permute-start(bf16[384]{0:T(512)(128)(2,1)S(1)} %get-tuple-element.699), channel_id=1, source_target_pairs={{0,4},{4,8},{8,12},{1,5},{5,9},{9,13},{2,6},{6,10},{10,14},{3,7},{... | collective-permute-start | bytes 2312 | tf_op jit(solution)/shard_map/while/body/eval_jaxpr/ppermute | solution.py:35
  13.7 13.0 %collective-permute-start.1 = (bf16[384,512]{0,1:T(8,128)(2,1)S(1)}, bf16[384,512]{0,1:T(8,128)(2,1)S(1)}, u32[]{:S(2)}, u32[]{:S(2)}) collective-permute-start(bf16[384,512]{0,1:T(8,128)(2,1)S(1)} %get-tuple-element.697), channel_id=1, source_target_pairs={{0,4},{4,8},{8,12},{1,5},{5,9},{9,13},{2,6},{6,10},{10,14},{3,7},{... | collective-permute-start | bytes 1179656 | tf_op jit(solution)/shard_map/while/body/eval_jaxpr/ppermute | solution.py:35
  17.2 16.6 %collective-permute-start.2 = (bf16[384,512]{0,1:T(8,128)(2,1)}, bf16[384,512]{0,1:T(8,128)(2,1)S(1)}, u32[]{:S(2)}, u32[]{:S(2)}) collective-permute-start(bf16[384,512]{0,1:T(8,128)(2,1)} %get-tuple-element.698), channel_id=1, source_target_pairs={{0,4},{4,8},{8,12},{1,5},{5,9},{9,13},{2,6},{6,10},{10,14},{3,7},{... | collective-permute-start | bytes 1179656 | tf_op jit(solution)/shard_map/while/body/eval_jaxpr/ppermute | solution.py:35
  35.7 10.0 %collective-permute-start = (bf16[384]{0:T(512)(128)(2,1)S(1)}, bf16[384]{0:T(512)(128)(2,1)S(1)}, u32[]{:S(2)}, u32[]{:S(2)}) collective-permute-start(bf16[384]{0:T(512)(128)(2,1)S(1)} %get-tuple-element.699), channel_id=1, source_target_pairs={{0,4},{4,8},{8,12},{1,5},{5,9},{9,13},{2,6},{6,10},{10,14},{3,7},{... | collective-permute-start | bytes 2312 | tf_op jit(solution)/shard_map/while/body/eval_jaxpr/ppermute | solution.py:35
  39.9 13.0 %collective-permute-start.1 = (bf16[384,512]{0,1:T(8,128)(2,1)S(1)}, bf16[384,512]{0,1:T(8,128)(2,1)S(1)}, u32[]{:S(2)}, u32[]{:S(2)}) collective-permute-start(bf16[384,512]{0,1:T(8,128)(2,1)S(1)} %get-tuple-element.697), channel_id=1, source_target_pairs={{0,4},{4,8},{8,12},{1,5},{5,9},{9,13},{2,6},{6,10},{10,14},{3,7},{... | collective-permute-start | bytes 1179656 | tf_op jit(solution)/shard_map/while/body/eval_jaxpr/ppermute | solution.py:35
  43.5 15.4 %collective-permute-start.2 = (bf16[384,512]{0,1:T(8,128)(2,1)}, bf16[384,512]{0,1:T(8,128)(2,1)S(1)}, u32[]{:S(2)}, u32[]{:S(2)}) collective-permute-start(bf16[384,512]{0,1:T(8,128)(2,1)} %get-tuple-element.698), channel_id=1, source_target_pairs={{0,4},{4,8},{8,12},{1,5},{5,9},{9,13},{2,6},{6,10},{10,14},{3,7},{... | collective-permute-start | bytes 1179656 | tf_op jit(solution)/shard_map/while/body/eval_jaxpr/ppermute | solution.py:35
  60.8 9.0 %collective-permute-start = (bf16[384]{0:T(512)(128)(2,1)S(1)}, bf16[384]{0:T(512)(128)(2,1)S(1)}, u32[]{:S(2)}, u32[]{:S(2)}) collective-permute-start(bf16[384]{0:T(512)(128)(2,1)S(1)} %get-tuple-element.699), channel_id=1, source_target_pairs={{0,4},{4,8},{8,12},{1,5},{5,9},{9,13},{2,6},{6,10},{10,14},{3,7},{... | collective-permute-start | bytes 2312 | tf_op jit(solution)/shard_map/while/body/eval_jaxpr/ppermute | solution.py:35
  65.1 12.0 %collective-permute-start.1 = (bf16[384,512]{0,1:T(8,128)(2,1)S(1)}, bf16[384,512]{0,1:T(8,128)(2,1)S(1)}, u32[]{:S(2)}, u32[]{:S(2)}) collective-permute-start(bf16[384,512]{0,1:T(8,128)(2,1)S(1)} %get-tuple-element.697), channel_id=1, source_target_pairs={{0,4},{4,8},{8,12},{1,5},{5,9},{9,13},{2,6},{6,10},{10,14},{3,7},{... | collective-permute-start | bytes 1179656 | tf_op jit(solution)/shard_map/while/body/eval_jaxpr/ppermute | solution.py:35
  67.6 14.6 %collective-permute-start.2 = (bf16[384,512]{0,1:T(8,128)(2,1)}, bf16[384,512]{0,1:T(8,128)(2,1)S(1)}, u32[]{:S(2)}, u32[]{:S(2)}) collective-permute-start(bf16[384,512]{0,1:T(8,128)(2,1)} %get-tuple-element.698), channel_id=1, source_target_pairs={{0,4},{4,8},{8,12},{1,5},{5,9},{9,13},{2,6},{6,10},{10,14},{3,7},{... | collective-permute-start | bytes 1179656 | tf_op jit(solution)/shard_map/while/body/eval_jaxpr/ppermute | solution.py:35
  84.1 1.7 %copy-start.2 = (bf16[384,512]{1,0:T(8,128)(2,1)S(1)}, bf16[384,512]{1,0:T(8,128)(2,1)}, u32[]{:S(2)}) copy-start(bf16[384,512]{1,0:T(8,128)(2,1)} %param.13) | copy-start | bytes 1179652
  85.8 18.9 %copy-start.6 = (u32[32]{0:T(128)S(1)}, u32[32]{0:T(128)}, u32[]{:S(2)}) copy-start(u32[32]{0:T(128)} %constant.136) | copy-start | bytes 388
where the time goes:
time: 130 us; the launch traced here: 129 us
  waiting for transfers between devices  34.3 us (26%)
  starting transfers between devices  31 us (24%)
  blocking collectives  25.6 us (20%)
  local copies, waits for them, and re-layouts  10.7 us (8%)
  matrix products  10.6 us (8%)
  loops' own time  8.13 us (6%)
  other arithmetic  7.61 us (6%)
  between operations  1.49 us (1%)
    ppermute x9, waiting for transfers between devices, shifted(): lax.ppermute(value, axis, [(source, source + steps) for source in range(i...  34.3 us
    ppermute x9, starting transfers between devices, shifted(): lax.ppermute(value, axis, [(source, source + steps) for source in range(i...  31 us
    all_gather x1, blocking collectives, entering(): lax.all_gather(part.astype(kind), axis)  15.7 us
    unnamed x1, blocking collectives  9.86 us
    another operation x1, loops' own time, entering(): return lax.fori_loop(0, devices, hop, start)  7.79 us
    unnamed x22, local copies, waits for them, and re-layouts  4.88 us
    dot_general x4, matrix products, one_block(): jnp.einsum('hts,shd->thd', expo.astype(jnp.bfloat16), value_block_slice,...  4.03 us
    dot_general x4, matrix products, one_block(): jnp.einsum('thd,shd->hts', q_heads, key_block_slice, preferred_element_ty...  3.59 us
  transfers between devices with their start and end apart: 9, of which 6 were waited for; matrix products, arithmetic and copies ran while one was open for 3% of the time, Pallas kernels for 0%

commit v1 on v0

v1 whole, which is shorter than its diff:
```python
import functools

import jax
import jax.numpy as jnp
from jax import lax
from jax.experimental import pallas as pl
from jax.experimental.pallas import tpu as pltpu
from jax.sharding import PartitionSpec as P

HEAD_DIM = 128
HIDDEN = -1e30
MESH = pl.DeviceIdType.MESH


def across(a, b):
    return lax.dot_general(a, b, (((1,), (1,)), ((), ())), preferred_element_type=jnp.float32)


def kernel(n, heads, reach, last_rows, q_lin, k_lin, v_lin, q_soft, k_soft, v_soft, seg,
           out_lin, out_soft, kbuf, vbuf, segbuf, state_in, state_out, bias, column, raw, top, total, accum,
           k_send, k_recv, v_send, v_recv, seg_send, seg_recv, state_send, state_recv):
    rows = q_lin.shape[0]
    me = lax.axis_index("seq")
    right, left = lax.rem(me + 1, n), lax.rem(me + n - 1, n)
    scale = HEAD_DIM ** (-0.5)

    def cols(h):
        return pl.ds(pl.multiple_of(h * HEAD_DIM, HEAD_DIM), HEAD_DIM)

    def first_row(d):
        return rows - last_rows if d == reach else 0

    def move(own, buf, send, recv, d, h):
        at = pl.ds(first_row(d), rows - first_row(d))
        source = own.at[at, cols(h)] if d == 1 else buf.at[d - 2, h, at, :]
        return pltpu.make_async_remote_copy(
            src_ref=source, dst_ref=buf.at[d - 1, h, at, :], send_sem=send.at[d - 1, h],
            recv_sem=recv.at[d - 1, h], device_id={"seq": right}, device_id_type=MESH)

    def key_move(d, h):
        return move(k_soft, kbuf, k_send, k_recv, d, h)

    def value_move(d, h):
        return move(v_soft, vbuf, v_send, v_recv, d, h)

    def seg_move(d):
        return pltpu.make_async_remote_copy(
            src_ref=seg if d == 1 else segbuf.at[d - 2], dst_ref=segbuf.at[d - 1], send_sem=seg_send.at[d - 1],
            recv_sem=seg_recv.at[d - 1], device_id={"seq": right}, device_id_type=MESH)

    def state_move():
        return pltpu.make_async_remote_copy(
            src_ref=state_out, dst_ref=state_in, send_sem=state_send,
            recv_sem=state_recv, device_id={"seq": right}, device_id_type=MESH)

    barrier = pltpu.get_barrier_semaphore()
    for neighbour in (left, right):
        pl.semaphore_signal(barrier, inc=1, device_id={"seq": neighbour}, device_id_type=MESH)
    pl.semaphore_wait(barrier, 2)

    @pl.when(me < n - 1)
    def _():
        seg_move(1).start()
        for h in range(heads):
            key_move(1, h).start()
            value_move(1, h).start()

    own_row = seg[...].astype(jnp.float32)
    column[...] = jnp.transpose(jnp.broadcast_to(own_row, (HEAD_DIM, rows)))
    own_last = own_row[:, rows - 1:]
    query = lax.broadcasted_iota(jnp.int32, (rows, rows), 0)
    key = lax.broadcasted_iota(jnp.int32, (rows, rows), 1)
    bias[...] = jnp.where((column[:, :1] == own_row) & (key <= query), 0.0, HIDDEN)

    def local(h, _):
        at = cols(h)
        scores = across(q_lin[:, at], k_lin[:, at])
        scores = jnp.where(bias[...] == 0.0, scores, 0.0).astype(jnp.bfloat16)
        raw[h] = jnp.dot(scores, v_lin[:, at], preferred_element_type=jnp.float32)
        logits = across(q_soft[:, at], k_soft[:, at]) * scale + bias[...]
        peak = jnp.max(logits, axis=-1, keepdims=True)
        expo = jnp.exp(logits - peak)
        top[h] = jnp.broadcast_to(peak, (rows, HEAD_DIM))
        total[h] = jnp.broadcast_to(jnp.sum(expo, axis=-1, keepdims=True), (rows, HEAD_DIM))
        accum[h] = jnp.dot(expo.astype(jnp.bfloat16), v_soft[:, at], preferred_element_type=jnp.float32)
        return 0

    lax.fori_loop(0, heads, local, 0)

    for d in range(1, reach + 1):
        begin = first_row(d)

        @pl.when(me >= d)
        def _(d=d, begin=begin):
            seg_move(d).wait_recv()
            if d < reach:
                @pl.when(me < n - 1)
                def _():
                    seg_move(d + 1).start()
            theirs = segbuf[d - 1].astype(jnp.float32)
            bias[...] = jnp.where(column[:, :1] == theirs, 0.0, HIDDEN)

            def block(h, _):
                key_move(d, h).wait_recv()
                if d < reach:
                    @pl.when(me < n - 1)
                    def _():
                        key_move(d + 1, h).start()
                value_move(d, h).wait_recv()
                if d < reach:
                    @pl.when(me < n - 1)
                    def _():
                        value_move(d + 1, h).start()
                at = cols(h)
                logits = across(q_soft[:, at], kbuf[d - 1, h, begin:, :]) * scale + bias[:, begin:]
                before = top[h]
                peak = jnp.maximum(before, jnp.max(logits, axis=-1, keepdims=True))
                factor = jnp.exp(before - peak)
                expo = jnp.exp(logits - peak[:, :1])
                top[h] = peak
                total[h] = total[h] * factor + jnp.sum(expo, axis=-1, keepdims=True)
                accum[h] = accum[h] * factor + jnp.dot(
                    expo.astype(jnp.bfloat16), vbuf[d - 1, h, begin:, :], preferred_element_type=jnp.float32)
                return 0

            lax.fori_loop(0, heads, block, 0)

    keep = jnp.where(column[...] == own_last, 1.0, 0.0)

    @pl.when(me == 0)
    def _():
        state_in[...] = jnp.zeros_like(state_in)
        segbuf[0] = jnp.full((1, rows), -1, jnp.int32)

    @pl.when(me > 0)
    def _():
        state_move().wait_recv()

    before_last = segbuf[0].astype(jnp.float32)[:, rows - 1:]

    @pl.when(me < n - 1)
    def _():
        going = jnp.where(before_last == own_last, 1.0, 0.0)
        for h in range(heads):
            at = cols(h)
            kept = (k_lin[:, at].astype(jnp.float32) * keep).astype(jnp.bfloat16)
            own = lax.dot_general(
                kept, v_lin[:, at], (((0,), (0,)), ((), ())), preferred_element_type=jnp.float32)
            state_out[h] = (own + going * state_in[h].astype(jnp.float32)).astype(jnp.bfloat16)
        state_move().start()

    apply = jnp.where(column[...] == before_last, 1.0, 0.0)
    for h in range(heads):
        at = cols(h)
        outer = jnp.dot(q_lin[:, at], state_in[h], preferred_element_type=jnp.float32)
        mixed = raw[h] + outer * apply
        norm = lax.rsqrt(jnp.mean(mixed * mixed, axis=-1, keepdims=True) + 1e-6)
        out_lin[:, at] = (mixed * norm).astype(jnp.bfloat16)
        out_soft[:, at] = (accum[h] / total[h]).astype(jnp.bfloat16)

    for d in range(1, reach + 1):
        @pl.when((me >= d - 1) & (me < n - 1))
        def _(d=d):
            seg_move(d).wait_send()

            def sent(h, _):
                key_move(d, h).wait_send()
                value_move(d, h).wait_send()
                return 0

            lax.fori_loop(0, heads, sent, 0)

    @pl.when(me < n - 1)
    def _():
        state_move().wait_send()


def solution(mesh):
    n = mesh.shape["seq"]

    def on_device(q_lin, k_lin, v_lin, q_soft, k_soft, v_soft, segment):
        rows, width = q_lin.shape
        heads = width // HEAD_DIM
        longest = rows * n * 5 // 8
        reach = min(n - 1, (longest - 2) // rows + 1)
        last_rows = min(rows, -(-(longest - 1 - (reach - 1) * rows) // 128) * 128)
        vmem = pl.BlockSpec(memory_space=pltpu.VMEM)
        dma = pltpu.SemaphoreType.DMA
        out = jax.ShapeDtypeStruct((rows, width), jnp.bfloat16)
        blocks = (heads, rows, HEAD_DIM)
        return pl.pallas_call(
            functools.partial(kernel, n, heads, reach, last_rows),
            out_shape=(out, out),
            in_specs=[vmem] * 7,
            out_specs=(vmem, vmem),
            scratch_shapes=[
                pltpu.VMEM((reach,) + blocks, jnp.bfloat16),
                pltpu.VMEM((reach,) + blocks, jnp.bfloat16),
                pltpu.VMEM((reach, 1, rows), jnp.int32),
                pltpu.VMEM((heads, HEAD_DIM, HEAD_DIM), jnp.bfloat16),
                pltpu.VMEM((heads, HEAD_DIM, HEAD_DIM), jnp.bfloat16),
                pltpu.VMEM((rows, rows), jnp.float32),
                pltpu.VMEM((rows, HEAD_DIM), jnp.float32),
                pltpu.VMEM(blocks, jnp.float32),
                pltpu.VMEM(blocks, jnp.float32),
                pltpu.VMEM(blocks, jnp.float32),
                pltpu.VMEM(blocks, jnp.float32),
                dma((reach, heads)), dma((reach, heads)), dma((reach, heads)), dma((reach, heads)),
                dma((reach,)), dma((reach,)), dma, dma,
            ],
            compiler_params=pltpu.CompilerParams(
                collective_id=0, has_side_effects=True, vmem_limit_bytes=56 * 1024 * 1024),
        )(q_lin, k_lin, v_lin, q_soft, k_soft, v_soft, segment.reshape(1, rows))

    tokens = P(("group", "seq"), "head")
    return jax.shard_map(
        on_device, mesh=mesh, in_specs=(tokens,) * 6 + (P(("group", "seq")),),
        out_specs=(tokens, tokens), check_vma=False)
```

time: 130 us -> 58.4 us (0.45)
  the two profiles are of different devices: /device:TPU:0 before, /device:TPU:28 now
where the time goes in v1:
time: 58.4 us; the launch traced here: 58.2 us
  Pallas kernels  53.7 us (92%)
  local copies, waits for them, and re-layouts  3.81 us (7%)
  between operations  0.65 us (1%)
    pallas_call x1, Pallas kernels, on_device(): pl.pallas_call(functools.partial(kernel, n, heads, reach, last_rows), out...  53.7 us
    unnamed x4, local copies, waits for them, and re-layouts  2.57 us
    reshape x1, local copies, waits for them, and re-layouts, on_device(): segment.reshape(1, rows)  1.25 us

profile of v1, /device:TPU:28, one launch (start us, length us, event | category | flops | bytes accessed | tf_op | source)
XLA Modules:
  0.0 58.2 jit_solution(675873838755703266)
XLA Ops:
  0.6 1.2 %reshape.7.seg = s32[1,384]{1,0:T(1,128)} reshape(s32[384]{0:T(512)} %param.13) | data formatting | bytes 3072 | tf_op jit(solution)/shard_map/reshape | solution.py:213
  1.9 53.7 %shard_map.86 = (bf16[384,512]{1,0:T(8,128)(2,1)}, bf16[384,512]{1,0:T(8,128)(2,1)}) custom-call(bf16[384,512]{1,0:T(8,128)(2,1)} %q_lin.1, bf16[384,512]{1,0:T(8,128)(2,1)} %k_lin.1, bf16[384,512]{1,0:T(8,128)(2,1)} %v_lin.1, bf16[384,512]{1,0:T(8,128)(2,1)} %q_soft.1, bf16[384,512]{1,0:T(8,128)(2,1)} %k_soft.1, bf16[384,512]{1,0:T(8,128)(2,1)} %v_soft.1, ...), custom_call_target="tpu_custom_call" | custom-call | tf_op jit(solution)/shard_map/pallas_call | solution.py:191
  55.6 0.0 copy-start
  55.6 1.8 %copy.11 = bf16[384,512]{1,0:T(8,128)(2,1)} copy(bf16[384,512]{1,0:T(8,128)(2,1)} %get-tuple-element.4) | data formatting | bytes 786432
  57.4 0.0 copy-done
  57.4 0.7 %copy.12 = bf16[384,512]{1,0:T(8,128)(2,1)} copy(bf16[384,512]{1,0:T(8,128)(2,1)S(1)} %copy-done) | data formatting | bytes 786432
Async XLA Ops:
  55.6 1.8 %copy-start = (bf16[384,512]{1,0:T(8,128)(2,1)S(1)}, bf16[384,512]{1,0:T(8,128)(2,1)}, u32[]{:S(2)}) copy-start(bf16[384,512]{1,0:T(8,128)(2,1)} %get-tuple-element.5) | copy-start | bytes 1179652
